TPU v7x, 32 devices: a whole 2x2x4 slice. The times are simulated.
32 devices in a mesh: segment: 4 (over y, x), seq: 8 (over z, core).
Axes of the slice: x: 2, y: 2, z: 4, core: 2. Of those that a mesh axis runs over, the one named last changes fastest.
Arguments:
- hidden: bfloat16 [4, 8192, 8192], P('segment', 'seq'), may hold values from -6 to 6
- span_lengths: int32 [4, 64], replicated, may hold values from 1 to 512, 8192 in all within a row
- section_of: int32 [4, 64], replicated, may hold values from 0 to 31
- section_live: int32 [32], P('seq'), may hold values 0 or 1
- w_in: bfloat16 [8192, 2048], P('seq'), may hold values from -0.5 to 0.5
- norm_gain: float32 [2048], replicated, may hold values from 0.5 to 1.5
- w_query: bfloat16 [2048, 2048], P(None, 'segment'), may hold values from -0.125 to 0.125
- w_key: bfloat16 [2048, 2048], P(None, 'segment'), may hold values from -0.125 to 0.125
- w_value: bfloat16 [2048, 2048], P(None, 'segment'), may hold values from -0.125 to 0.125
- w_out: bfloat16 [2048, 2048], P('segment'), may hold values from -0.125 to 0.125
Outputs:
- section_out: bfloat16 [32, 2048], P('seq')
All inputs are finite; a program needn't handle non-finite values. No bound on the sum of `section_live` on one device may be relied on, other than what follows from the above.
Results may differ from a plain program's by a relative error of at most 0.007.
Values may be sent and summed in bfloat16 or wider, within the bound.
A program may use at most 128 MiB of HBM per device.

v0:
```python
import jax
import jax.numpy as jnp
from jax import lax
from jax.sharding import PartitionSpec as P

HEAD_DIM = 128


def shards(
    hidden, span_lengths, section_of, section_live, w_in, norm_gain, w_query, w_key, w_value, w_out
):
    tokens = hidden[0]
    seq_count = lax.axis_size("seq")
    seq_index = lax.axis_index("seq")
    segment_index = lax.axis_index("segment")
    tok_count = tokens.shape[0]
    lengths = lax.dynamic_index_in_dim(span_lengths, segment_index, 0, keepdims=False)
    span_ends = jnp.cumsum(lengths)
    span_starts = span_ends - lengths
    positions = seq_index * tok_count + jnp.arange(tok_count, dtype=jnp.int32)
    member = (
        (positions[None, :] >= span_starts[:, None]) & (positions[None, :] < span_ends[:, None])
    ).astype(jnp.bfloat16)
    partial_value = jnp.dot(member, tokens, preferred_element_type=jnp.float32)
    length_float = lengths.astype(jnp.float32)
    sections_here = section_live.shape[0]
    section_total = sections_here * seq_count
    section_ids = jnp.arange(section_total, dtype=jnp.int32)
    own_sections = seq_index * sections_here + jnp.arange(sections_here, dtype=jnp.int32)
    flat_sections = section_of.reshape(-1)
    count_all = jnp.sum(
        (section_ids[:, None] == flat_sections[None, :]).astype(jnp.float32), axis=1
    )
    doc_sections = lax.dynamic_index_in_dim(section_of, segment_index, 0, keepdims=False)
    weighted = partial_value / length_float[:, None]
    doc_onehot = (section_ids[:, None] == doc_sections[None, :]).astype(jnp.float32)
    section_part = jnp.dot(doc_onehot, weighted, precision=lax.Precision.HIGHEST)
    feature_block = lax.psum_scatter(section_part, "seq", scatter_dimension=1, tiled=True)
    doc_total = lax.psum(feature_block, "segment")
    pooled = (doc_total / jnp.maximum(count_all, 1.0)[:, None]).astype(jnp.bfloat16)
    projected = jnp.dot(pooled, w_in, preferred_element_type=jnp.float32)
    section_in = lax.psum_scatter(projected, "seq", scatter_dimension=0, tiled=True)
    scale = lax.rsqrt(jnp.mean(section_in * section_in, axis=1, keepdims=True) + 1e-05)
    normed = (section_in * scale * norm_gain[None, :]).astype(jnp.bfloat16)
    queries = jnp.dot(normed, w_query, preferred_element_type=jnp.float32).astype(jnp.bfloat16)
    keys_here = jnp.dot(normed, w_key, preferred_element_type=jnp.float32).astype(jnp.bfloat16)
    values_here = jnp.dot(normed, w_value, preferred_element_type=jnp.float32).astype(jnp.bfloat16)
    live_here = section_live.astype(jnp.bfloat16)
    keys_all, values_all, live_all = (
        lax.all_gather(keys_here, "seq", axis=0, tiled=True),
        lax.all_gather(values_here, "seq", axis=0, tiled=True),
        lax.all_gather(live_here, "seq", axis=0, tiled=True),
    )
    local_heads = queries.shape[1] // HEAD_DIM
    query_heads = queries.reshape(sections_here, local_heads, HEAD_DIM)
    key_heads = keys_all.reshape(section_total, local_heads, HEAD_DIM)
    value_heads = values_all.reshape(section_total, local_heads, HEAD_DIM)
    scores = jnp.einsum("qhd,khd->hqk", query_heads, key_heads, preferred_element_type=jnp.float32)
    scores = scores / jnp.sqrt(jnp.float32(HEAD_DIM))
    allowed = (live_all[None, :] > 0) | (section_ids[None, :] == own_sections[:, None])
    scores = jnp.where(allowed[None, :, :], scores, jnp.float32(-1e30))
    probs = jax.nn.softmax(scores, axis=-1).astype(jnp.bfloat16)
    attended = jnp.einsum(
        "hqk,khd->qhd", probs, value_heads, preferred_element_type=jnp.float32
    ).astype(jnp.bfloat16)
    attended = attended.reshape(sections_here, local_heads * HEAD_DIM)
    head_terms = jnp.dot(attended, w_out, preferred_element_type=jnp.float32)
    combined = lax.psum(head_terms, "segment")
    return (section_in + combined).astype(jnp.bfloat16)


def solution(mesh):
    in_specs = (
        P("segment", "seq", None),
        P(),
        P(),
        P("seq"),
        P("seq", None),
        P(),
        P(None, "segment"),
        P(None, "segment"),
        P(None, "segment"),
        P("segment", None),
    )
    out_specs = P("seq", None)
    return jax.shard_map(shards, mesh=mesh, in_specs=in_specs, out_specs=out_specs, check_vma=False)
```

profile of v0, /device:TPU:0, one launch (start us, length us, event | category | flops | bytes accessed | tf_op | source)
XLA Modules:
  0.0 217.7 jit_solution(10877947771555918930)
XLA Ops:
  6.5 0.9 fusion.30
  7.4 0.1 copy.25
  7.5 0.1 reduce-window.7
  7.6 0.1 reduce
  7.7 0.7 bitcast_subtract_fusion
  8.4 8.8 %fusion.3 = f32[64,8192]{1,0:T(8,128)S(1)} fusion(bf16[1,1024,8192]{2,1,0:T(8,128)(2,1)} %param.10, f32[64]{0:T(128)S(1)} %get-tuple-element.6, s32[1024]{0:T(1024)S(1)} %iota_add_fusion, s32[64]{0:T(128)S(1)} %reduce, s32[64]{0:T(128)S(1)} %bitcast_subtract_fusion), kind=kOutput, calls=%fused_computation.3 | convolution fusion | flops 1074462720 | bytes 18879232 | tf_op jit(solution)/shard_map/dot_general | solution.py:24
  17.3 1.8 fusion.25
  19.1 0.0 reduce-scatter.2.cloned.1.call-update
  19.1 0.0 all-reduce.5.cloned.1.call-start
  19.2 0.1 eq.52
  19.3 0.7 fusion.31
  20.6 0.2 dynamic-update-slice
  20.9 18.2 %all-reduce = bf16[32]{0:T(256)(128)(2,1)S(1)} all-reduce(bf16[32]{0:T(256)(128)(2,1)S(1)} %dynamic-update-slice), channel_id=1, replica_groups=mesh['segment'=4,'seq'=8] {'seq'}, use_global_device_ids=true, to_apply=%add | all-reduce | flops 32 | bytes 128
  39.1 0.1 convert_reduce_fusion
  39.2 15.9 %reduce-scatter.2.cloned.1.call-done = f32[32,1024]{1,0:T(8,128)} async-done(((f32[32,8192]{1,0:T(8,128)}), f32[32,1024]{1,0:T(8,128)}) %reduce-scatter.2.cloned.1.call-update) | async-done | bytes 131088 | tf_op jit(solution)/shard_map/reduce_scatter | solution.py:38
  55.1 0.0 all-reduce.5.cloned.1.call-update
  55.1 0.0 all-reduce.7.cloned.1.call-start
  55.8 42.1 %all-reduce.5.cloned.1.call-done = f32[32,1024]{1,0:T(8,128)} async-done(((f32[32,1024]{1,0:T(8,128)}), f32[32,1024]{1,0:T(8,128)}) %all-reduce.5.cloned.1.call-update) | async-done | bytes 131088 | tf_op jit(solution)/shard_map/psum | solution.py:39
  97.9 3.8 %fusion.20 = f32[32,2048]{1,0:T(8,128)} fusion(bf16[1024,2048]{1,0:T(8,128)(2,1)} %param.14, f32[32,1024]{1,0:T(8,128)} %all-reduce.5.cloned.1.call-done, f32[32]{0:T(128)S(1)} %broadcast_maximum_fusion), kind=kOutput, calls=%fused_computation.24 | convolution fusion | flops 134283264 | bytes 4587648 | tf_op jit(solution)/shard_map/dot_general | solution.py:41
  101.7 0.0 all-reduce.7.cloned.1.call-update
  101.7 0.1 fusion.29
  101.8 55.5 %all-reduce.7.cloned.1.call-done = f32[32,2048]{1,0:T(8,128)} async-done(((f32[32,2048]{1,0:T(8,128)}), f32[32,2048]{1,0:T(8,128)}) %all-reduce.7.cloned.1.call-update) | async-done | bytes 262160
  157.3 1.0 multiply_reduce_fusion
  158.3 2.0 fusion.11
  160.3 14.1 %all-gather.1 = bf16[8,4,512]{2,1,0:T(4,128)(2,1)S(1)} all-gather(bf16[1,4,512]{2,1,0:T(4,128)(2,1)S(1)} %fusion.11), channel_id=1, replica_groups=mesh['segment'=4,'seq'=8] {'seq'}, dimensions={0}, use_global_device_ids=true | all-gather | bytes 36864 | tf_op jit(solution)/shard_map/all_gather | solution.py:50
  174.4 2.2 fusion.8
  176.6 0.2 fusion.32
  176.8 2.1 fusion.9
  178.8 14.1 %all-gather = bf16[8,4,512]{2,1,0:T(4,128)(2,1)S(1)} all-gather(bf16[1,4,512]{2,1,0:T(4,128)(2,1)S(1)} %fusion.9), channel_id=1, replica_groups=mesh['segment'=4,'seq'=8] {'seq'}, dimensions={0}, use_global_device_ids=true | all-gather | bytes 36864 | tf_op jit(solution)/shard_map/all_gather | solution.py:51
  193.0 0.5 fusion.13
  193.5 16.2 %psum.15 = f32[4,2048]{1,0:T(4,128)S(1)} all-reduce(f32[4,2048]{1,0:T(4,128)S(1)} %fusion.13), channel_id=1, replica_groups=mesh['segment'=4,'seq'=8] {'segment'}, use_global_device_ids=true, to_apply=%region_8.9 | all-reduce | flops 8192 | bytes 65536 | tf_op jit(solution)/shard_map/psum | solution.py:68
  209.7 1.5 add_convert_fusion
  (20 shorter events, 0.1 us)
Async XLA Ops:
  6.5 186.4 %copy-start = (bf16[512,2048]{1,0:T(8,128)(2,1)S(1)}, bf16[512,2048]{1,0:T(8,128)(2,1)}, u32[]{:S(2)}) copy-start(bf16[512,2048]{1,0:T(8,128)(2,1)} %param.19) | copy-start | bytes 6291460
  6.5 48.5 %reduce-scatter.2.cloned.1.call-start = ((), (), s32[]{:S(2)}) async-start(), calls=%async_computation.1 | async-start | bytes 1179648 | tf_op jit(solution)/shard_map/reduce_scatter | solution.py:38
  17.3 1.9 copy-start.2
  17.3 2.0 copy-start.4
  17.3 2.0 copy-start.3
  19.1 78.7 %all-reduce.5.cloned.1.call-start = ((), (), s32[]{:S(2)}) async-start(), calls=%async_computation.2 | async-start | bytes 262144 | tf_op jit(solution)/shard_map/psum | solution.py:39
  55.1 102.2 %all-reduce.7.cloned.1.call-start = ((), (), s32[]{:S(2)}) async-start(), calls=%async_computation.3 | async-start | bytes 524288
  55.8 102.5 %copy-start.1 = (f32[2048]{0:T(1024)S(1)}, f32[2048]{0:T(1024)}, u32[]{:S(2)}) copy-start(f32[2048]{0:T(1024)} %param.15) | copy-start | bytes 24580
Sparse Core Ops, SparseCore 0:
  19.3 35.7 reduce-scatter.1
  58.0 39.8 all-reduce.4
  101.9 55.4 all-reduce.6
where the time goes:
time: 218 us
  waiting for transfers between devices  113 us (52%)
  blocking collectives  62.6 us (29%)
  matrix products  21.3 us (10%)
  between operations  14.5 us (7%)
  other arithmetic  4.58 us (2%)
    unnamed x4, waiting for transfers between devices  55.5 us
    psum x1, waiting for transfers between devices, shards(): doc_total = lax.psum(feature_block, 'segment')  42.1 us
    unnamed x1, blocking collectives  18.2 us
    psum x1, blocking collectives, shards(): combined = lax.psum(head_terms, 'segment')  16.2 us
    reduce_scatter x1, waiting for transfers between devices, shards(): lax.psum_scatter(section_part, 'seq', scatter_dimension=1, tiled=True)  15.9 us
    all_gather x1, blocking collectives, shards(): lax.all_gather(keys_here, 'seq', axis=0, tiled=True)  14.1 us
    all_gather x1, blocking collectives, shards(): lax.all_gather(values_here, 'seq', axis=0, tiled=True)  14.1 us
    dot_general x1, matrix products, shards(): partial_value = jnp.dot(member, tokens, preferred_element_type=jnp.float32)  8.85 us
  transfers between devices with their start and end apart: 3, of which 3 were waited for; matrix products, arithmetic and copies ran while one was open for 1% of the time, Pallas kernels for 0%

commit v1 on v0

v1 whole, which is shorter than its diff:
```python
import functools
import jax
import jax.numpy as jnp
from jax import lax
from jax.experimental import pallas as pl
from jax.experimental.pallas import tpu as pltpu
from jax.sharding import PartitionSpec as P

HEAD_DIM = 128
MESH = pl.DeviceIdType.MESH
AHEAD = 4


def kernel(
    seg_n, seq_n,
    hidden, lengths_ref, sections_ref, live_ref, gain_ref, w_in, w_query, w_key, w_value, w_out,
    out_ref,
    hid, win, wqkv, wout, weights, pair_send, pair_recv, seg_own, seg_send, seg_recv,
    line_send, line_recv, pooled, proj_send, proj_recv, kv_send, kv_recv, kv_all,
    term_recv,
    load_sem, pair_ss, pair_rs, seg_ss, seg_rs, line_ss, line_rs, pool_ss, pool_rs,
    proj_ss, proj_rs, kv_ss, kv_rs, term_ss, term_rs,
):
    seg = lax.axis_index("segment")
    q = lax.axis_index("seq")
    core = lax.rem(q, 2)
    chip = lax.div(q, 2)
    chips = seq_n // 2
    partner = q + 1 - 2 * core
    tokens = hidden.shape[1]
    features = hid.shape[2]
    sub = features // seg_n
    here = live_ref.shape[0]
    sections = here * seq_n
    docs, spans = lengths_ref.shape
    f32, bf16 = jnp.float32, jnp.bfloat16

    def seg_peer(d):
        return lax.rem(seg + d, seg_n)

    def seq_peer(d):
        return lax.rem(q + d, seq_n)

    def dest_chip(k):
        return lax.rem(chip + 1 + k, chips)

    order = [("peer", 0)]
    for k in range(1, chips):
        order += [("peer", k), ("own", k - 1)]
    order.append(("own", chips - 1))

    def load(i):
        kind, k = order[i]
        block = dest_chip(k) * 2 + (core if kind == "own" else 1 - core)
        return pltpu.make_async_copy(
            hidden.at[0, :, pl.ds(pl.multiple_of(block * features, 128), features)],
            hid.at[i],
            load_sem.at[i],
        )

    n = len(order)
    weight_loads = [
        pltpu.make_async_copy(w_in, win, load_sem.at[n]),
        pltpu.make_async_copy(w_query, wqkv.at[0], load_sem.at[n + 1]),
        pltpu.make_async_copy(w_key, wqkv.at[1], load_sem.at[n + 2]),
        pltpu.make_async_copy(w_value, wqkv.at[2], load_sem.at[n + 3]),
        pltpu.make_async_copy(w_out, wout, load_sem.at[n + 4]),
    ]
    for i in range(min(AHEAD, n)):
        load(i).start()

    barrier = pltpu.get_barrier_semaphore()
    for d in range(1, seg_n):
        pl.semaphore_signal(barrier, inc=1, device_id=(seg_peer(d), q), device_id_type=MESH)
    for d in range(1, seq_n):
        pl.semaphore_signal(barrier, inc=1, device_id=(seg, seq_peer(d)), device_id_type=MESH)

    len_row = lengths_ref[pl.ds(seg, 1), :].astype(f32)
    sec_row = sections_ref[pl.ds(seg, 1), :]
    c_row = lax.broadcasted_iota(jnp.int32, (spans, spans), 0)
    c_col = lax.broadcasted_iota(jnp.int32, (spans, spans), 1)
    len_all = jnp.broadcast_to(len_row, (spans, spans))
    ends = jnp.sum(jnp.where(c_col <= c_row, len_all, 0.0), axis=1, keepdims=True)
    starts = jnp.sum(jnp.where(c_col < c_row, len_all, 0.0), axis=1, keepdims=True)
    position = (q * tokens + lax.broadcasted_iota(jnp.int32, (spans, tokens), 1)).astype(f32)
    member = jnp.where((position >= starts) & (position < ends), 1.0, 0.0).astype(bf16)
    inverse = 1.0 / len_row
    high = inverse.astype(bf16).astype(f32)
    low = inverse - high
    onehot = lax.broadcasted_iota(jnp.int32, (sections, spans), 0) == sec_row
    for t, part in enumerate((high, low)):
        spread = jnp.where(onehot, jnp.broadcast_to(part, (sections, spans)), 0.0).astype(bf16)
        weights[pl.ds(t * sections, sections), :] = jnp.dot(
            spread, member, preferred_element_type=f32
        ).astype(bf16)
    count = jnp.zeros((sections, 1), f32)
    for d in range(docs):
        same = lax.broadcasted_iota(jnp.int32, (sections, spans), 0) == sections_ref[d : d + 1, :]
        count += jnp.sum(jnp.where(same, 1.0, 0.0), axis=1, keepdims=True)
    count = jnp.maximum(count, 1.0)

    def pair_copy(k):
        return pltpu.make_async_remote_copy(
            pair_send.at[k], pair_recv.at[k], pair_ss.at[k], pair_rs.at[k],
            device_id=(seg, partner), device_id_type=MESH)

    def seg_copy(k, d):
        return pltpu.make_async_remote_copy(
            seg_send.at[k, seg_peer(d)], seg_recv.at[k, d - 1],
            seg_ss.at[k, d - 1], seg_rs.at[k, d - 1],
            device_id=(seg_peer(d), q), device_id_type=MESH)

    def line_copy(k):
        return pltpu.make_async_remote_copy(
            line_send.at[k], line_recv.at[k], line_ss.at[k], line_rs.at[k],
            device_id=(seg, dest_chip(k) * 2 + core), device_id_type=MESH)

    def seg_total(k):
        total = seg_own[k, seg]
        for d in range(1, seg_n):
            seg_copy(k, d).wait_recv()
            total += seg_recv[k, d - 1].astype(f32)
        return total

    for i, (kind, k) in enumerate(order):
        if i + AHEAD < n:
            load(i + AHEAD).start()
        elif i + AHEAD == n:
            for w in weight_loads:
                w.start()
        load(i).wait()
        both = jnp.dot(weights[...], hid[i], preferred_element_type=f32)
        part = both[:sections] + both[sections:]
        if i == 0:
            pl.semaphore_wait(barrier, seg_n + seq_n - 2)
        if kind == "peer":
            pair_send[k] = part
            pair_copy(k).start()
            continue
        pair_copy(k).wait_recv()
        part = part + pair_recv[k]
        for s in range(seg_n):
            piece = part[:, s * sub : (s + 1) * sub]
            seg_own[k, s] = piece
            seg_send[k, s] = piece.astype(bf16)
        for d in range(1, seg_n):
            seg_copy(k, d).start()
        if k > 0:
            line_send[k - 1] = seg_total(k - 1).astype(bf16)
            line_copy(k - 1).start()

    total = seg_total(chips - 1)
    for k in range(chips - 1):
        line_copy(k).wait_recv()
        total += line_recv[k].astype(f32)
    pooled[seg] = (total / count).astype(bf16)

    def pool_copy(d):
        return pltpu.make_async_remote_copy(
            pooled.at[seg], pooled.at[seg], pool_ss.at[d - 1], pool_rs.at[d - 1],
            device_id=(seg_peer(d), q), device_id_type=MESH)

    for d in range(1, seg_n):
        pool_copy(d).start()
    weight_loads[0].wait()
    for d in range(1, seg_n):
        pool_copy(d).wait_recv()
    projected = jnp.dot(pooled[0], win[0:sub, :], preferred_element_type=f32)
    for s in range(1, seg_n):
        projected += jnp.dot(
            pooled[s], win[s * sub : (s + 1) * sub, :], preferred_element_type=f32)
    for s in range(seq_n):
        proj_send[s] = projected[s * here : (s + 1) * here, :].astype(bf16)

    def proj_copy(d):
        return pltpu.make_async_remote_copy(
            proj_send.at[seq_peer(d)], proj_recv.at[q], proj_ss.at[d - 1], proj_rs.at[d - 1],
            device_id=(seg, seq_peer(d)), device_id_type=MESH)

    for d in range(1, seq_n):
        proj_copy(d).start()
    proj_recv[q] = proj_send[q]
    for w in weight_loads[1:]:
        w.wait()
    for d in range(1, seq_n):
        proj_copy(d).wait_recv()
    section_in = proj_recv[0].astype(f32)
    for s in range(1, seq_n):
        section_in += proj_recv[s].astype(f32)
    scale = lax.rsqrt(jnp.mean(section_in * section_in, axis=1, keepdims=True) + 1e-05)
    normed = (section_in * scale * gain_ref[...]).astype(bf16)
    columns = wqkv.shape[2]
    kv_send[:, 0:columns] = jnp.dot(normed, wqkv[1], preferred_element_type=f32).astype(bf16)
    kv_send[:, columns : 2 * columns] = jnp.dot(
        normed, wqkv[2], preferred_element_type=f32).astype(bf16)
    row = lax.broadcasted_iota(jnp.int32, (here, HEAD_DIM), 0)
    live = jnp.zeros((here, HEAD_DIM), f32)
    for i in range(here):
        live = jnp.where(row == i, live_ref[i].astype(f32), live)
    kv_send[:, 2 * columns :] = live.astype(bf16)

    def kv_copy(d):
        return pltpu.make_async_remote_copy(
            kv_send, kv_recv.at[q], kv_ss.at[d - 1], kv_rs.at[d - 1],
            device_id=(seg, seq_peer(d)), device_id_type=MESH)

    for d in range(1, seq_n):
        kv_copy(d).start()
    kv_recv[q] = kv_send[...]
    queries = jnp.dot(normed, wqkv[0], preferred_element_type=f32).astype(bf16)
    for d in range(1, seq_n):
        kv_copy(d).wait_recv()
    for s in range(seq_n):
        kv_all[s * here : (s + 1) * here, :] = kv_recv[s].astype(f32)
    across = (((1,), (1,)), ((), ()))
    live_all = kv_all[:, 2 * columns :].astype(bf16)
    live_sum = lax.dot_general(
        jnp.ones((here, HEAD_DIM), bf16), live_all, across, preferred_element_type=f32)
    own = q * here + lax.broadcasted_iota(jnp.int32, (here, sections), 0)
    allowed = (live_sum > 0) | (lax.broadcasted_iota(jnp.int32, (here, sections), 1) == own)
    terms = jnp.zeros((here, wout.shape[1]), f32)
    attended = []
    for h in range(columns // HEAD_DIM):
        lo = h * HEAD_DIM
        keys = kv_all[:, lo : lo + HEAD_DIM].astype(bf16)
        values = kv_all[:, columns + lo : columns + lo + HEAD_DIM].astype(bf16)
        scores = lax.dot_general(
            queries[:, lo : lo + HEAD_DIM], keys, across, preferred_element_type=f32)
        scores = jnp.where(allowed, scores / jnp.sqrt(f32(HEAD_DIM)), f32(-1e30))
        grown = jnp.exp(scores - jnp.max(scores, axis=1, keepdims=True))
        probs = (grown / jnp.sum(grown, axis=1, keepdims=True)).astype(bf16)
        attended.append(jnp.dot(probs, values, preferred_element_type=f32).astype(bf16))
    terms = jnp.dot(
        jnp.concatenate(attended, axis=1), wout[...], preferred_element_type=f32)
    term_recv[seg] = terms

    def term_copy(d):
        return pltpu.make_async_remote_copy(
            term_recv.at[seg], term_recv.at[seg], term_ss.at[d - 1], term_rs.at[d - 1],
            device_id=(seg_peer(d), q), device_id_type=MESH)

    for d in range(1, seg_n):
        term_copy(d).start()
    for d in range(1, seg_n):
        term_copy(d).wait_recv()
    combined = term_recv[0]
    for s in range(1, seg_n):
        combined += term_recv[s]
    out_ref[...] = (section_in + combined).astype(out_ref.dtype)

    for k in range(chips):
        pair_copy(k).wait_send()
        for d in range(1, seg_n):
            seg_copy(k, d).wait_send()
        if k < chips - 1:
            line_copy(k).wait_send()
    for d in range(1, seg_n):
        pool_copy(d).wait_send()
        term_copy(d).wait_send()
    for d in range(1, seq_n):
        proj_copy(d).wait_send()
        kv_copy(d).wait_send()


def shards(
    hidden, span_lengths, section_of, section_live, w_in, norm_gain, w_query, w_key, w_value, w_out
):
    seg_n, seq_n = lax.axis_size("segment"), lax.axis_size("seq")
    tokens, depth = hidden.shape[1:]
    here = section_live.shape[0]
    sections = here * seq_n
    chips = seq_n // 2
    features = depth // seq_n
    sub = features // seg_n
    width, columns = w_query.shape
    bf16, f32 = jnp.bfloat16, jnp.float32
    vmem = pl.BlockSpec(memory_space=pltpu.VMEM)
    smem = pl.BlockSpec(memory_space=pltpu.SMEM)
    hbm = pl.BlockSpec(memory_space=pl.ANY)
    dma = pltpu.SemaphoreType.DMA
    kv = 2 * columns + HEAD_DIM
    return pl.pallas_call(
        functools.partial(kernel, seg_n, seq_n),
        out_shape=jax.ShapeDtypeStruct((here, width), bf16),
        in_specs=[hbm, vmem, vmem, smem, vmem, hbm, hbm, hbm, hbm, hbm],
        out_specs=vmem,
        scratch_shapes=[
            pltpu.VMEM((seq_n, tokens, features), bf16),
            pltpu.VMEM(w_in.shape, bf16),
            pltpu.VMEM((3, width, columns), bf16),
            pltpu.VMEM(w_out.shape, bf16),
            pltpu.VMEM((2 * sections, tokens), bf16),
            pltpu.VMEM((chips, sections, features), f32),
            pltpu.VMEM((chips, sections, features), f32),
            pltpu.VMEM((chips, seg_n, sections, sub), f32),
            pltpu.VMEM((chips, seg_n, sections, sub), bf16),
            pltpu.VMEM((chips, seg_n - 1, sections, sub), bf16),
            pltpu.VMEM((chips - 1, sections, sub), bf16),
            pltpu.VMEM((chips - 1, sections, sub), bf16),
            pltpu.VMEM((seg_n, sections, sub), bf16),
            pltpu.VMEM((seq_n, here, width), bf16),
            pltpu.VMEM((seq_n, here, width), bf16),
            pltpu.VMEM((here, kv), bf16),
            pltpu.VMEM((seq_n, here, kv), bf16),
            pltpu.VMEM((sections, kv), f32),
            pltpu.VMEM((seg_n, here, width), f32),
            dma((seq_n + 5,)),
            dma((chips,)), dma((chips,)),
            dma((chips, seg_n - 1)), dma((chips, seg_n - 1)),
            dma((chips - 1,)), dma((chips - 1,)),
            dma((seg_n - 1,)), dma((seg_n - 1,)),
            dma((seq_n - 1,)), dma((seq_n - 1,)),
            dma((seq_n - 1,)), dma((seq_n - 1,)),
            dma((seg_n - 1,)), dma((seg_n - 1,)),
        ],
        compiler_params=pltpu.CompilerParams(
            collective_id=0, has_side_effects=True, vmem_limit_bytes=60 * 1024 * 1024
        ),
    )(
        hidden, span_lengths, section_of, section_live, norm_gain.reshape(1, -1),
        w_in, w_query, w_key, w_value, w_out,
    )


def solution(mesh):
    in_specs = (
        P("segment", "seq", None),
        P(),
        P(),
        P("seq"),
        P("seq", None),
        P(),
        P(None, "segment"),
        P(None, "segment"),
        P(None, "segment"),
        P("segment", None),
    )
    out_specs = P("seq", None)
    return jax.shard_map(shards, mesh=mesh, in_specs=in_specs, out_specs=out_specs, check_vma=False)
```

time: 218 us -> 38.7 us (0.18)
  waiting for transfers between devices: 113 us -> 0 us
  blocking collectives: 62.6 us -> 0 us
  Pallas kernels: 0 us -> 37.1 us
  matrix products: 21.3 us -> 0 us
  between operations: 14.5 us -> 0.01 us
  other arithmetic: 4.58 us -> 0 us
    unnamed x4 -> x0, waiting for transfers between devices: 55.5 us -> none
    psum x1 -> x0, waiting for transfers between devices: 42.1 us -> none  [shards(): doc_total = lax.psum(feature_block, 'segment')]
    pallas_call x0 -> x1, Pallas kernels: none -> 37.1 us  [shards(): pl.pallas_call(functools.partial(kernel, seg_n, seq_n), out_shape=jax.Sha...]
    all_gather x2 -> x0, blocking collectives: 28.2 us -> none  [the longest x1 14.1 us: shards(): lax.all_gather(keys_here, 'seq', axis=0, tiled=True)]
    dot_general x7 -> x0, matrix products: 21.3 us -> none  [the longest x1 8.85 us: shards(): partial_value = jnp.dot(member, tokens, preferred_element_type=jnp.float32)]
    unnamed x1 -> x0, blocking collectives: 18.2 us -> none
    psum x1 -> x0, blocking collectives: 16.2 us -> none  [shards(): combined = lax.psum(head_terms, 'segment')]
    reduce_scatter x1 -> x0, waiting for transfers between devices: 15.9 us -> none  [shards(): lax.psum_scatter(section_part, 'seq', scatter_dimension=1, tiled=True)]
  transfers between devices with their start and end apart: 3 -> 0, of which waited for: 3 -> 0; matrix products, arithmetic and copies ran while one was open for 1% -> 0% of each run, Pallas kernels for 0% -> 0%
where the time goes in v1:
time: 38.7 us; the launch traced here: 38.4 us
  Pallas kernels  37.1 us (96%)
  local copies, waits for them, and re-layouts  1.33 us (3%)
    pallas_call x1, Pallas kernels, shards(): pl.pallas_call(functools.partial(kernel, seg_n, seq_n), out_shape=jax.Sha...  37.1 us
    unnamed x1, local copies, waits for them, and re-layouts  1.33 us

profile of v1, /device:TPU:0, one launch (start us, length us, event | category | flops | bytes accessed | tf_op | source)
XLA Modules:
  0.0 38.4 jit_solution(1649639896770216313)
XLA Ops:
  0.0 37.1 %shard_map.100 = bf16[4,2048]{1,0:T(4,128)(2,1)} custom-call(bf16[1,1024,8192]{2,1,0:T(8,128)(2,1)} %hidden.1, s32[4,64]{1,0:T(4,128)} %lengths_ref.1, s32[4,64]{1,0:T(4,128)} %sections_ref.1, s32[4]{0:T(128)} %live_ref.1, f32[1,2048]{1,0:T(1,128)} %bitcast.1, bf16[1024,2048]{1,0:T(8,128)(2,1)} %w_in.1, bf16[2048,512]{1,0:T(8,128)(2,1)} %w_query.1, ...), custom_call_target="tpu_custom_call" | custom-call | tf_op jit(solution)/shard_map/pallas_call | solution.py:282
  37.1 1.3 %copy.12 = bf16[4,2048]{1,0:T(4,128)(2,1)} copy(bf16[4,2048]{1,0:T(4,128)(2,1)} %shard_map.100) | data formatting | bytes 32768

commit v2 on v1

--- a/solution.py
+++ b/solution.py
@@ -8,14 +8,13 @@
 
 HEAD_DIM = 128
 MESH = pl.DeviceIdType.MESH
-AHEAD = 4
 
 
 def kernel(
     seg_n, seq_n,
-    hidden, lengths_ref, sections_ref, live_ref, gain_ref, w_in, w_query, w_key, w_value, w_out,
+    hidden, lengths_in, sections_in, live_in, gain_in, w_in, w_query, w_key, w_value, w_out,
     out_ref,
-    hid, win, wqkv, wout, weights, pair_send, pair_recv, seg_own, seg_send, seg_recv,
+    lengths_ref, sections_ref, live_ref, gain_ref, hid, win, wqkv, wout, product, weights, pair_send, pair_recv, seg_own, seg_send, seg_recv,
     line_send, line_recv, pooled, proj_send, proj_recv, kv_send, kv_recv, kv_all,
     term_recv,
     load_sem, pair_ss, pair_rs, seg_ss, seg_rs, line_ss, line_rs, pool_ss, pool_rs,
@@ -41,13 +40,24 @@
     def seq_peer(d):
         return lax.rem(q + d, seq_n)
 
+    upper = lax.div(chip, max(chips // 2, 1))
+    far_first = []
+    for i in range(1, chips):
+        k = upper * i + (1 - upper) * (chips - i)
+        for c in range(2):
+            far_first.append(lax.rem(lax.rem(chip + k, chips) * 2 + c - q + seq_n, seq_n))
+    far_first.append(lax.rem(partner - q + seq_n, seq_n))
+
     def dest_chip(k):
         return lax.rem(chip + 1 + k, chips)
 
-    order = [("peer", 0)]
-    for k in range(1, chips):
-        order += [("peer", k), ("own", k - 1)]
-    order.append(("own", chips - 1))
+    barrier = pltpu.get_barrier_semaphore()
+    for d in range(1, seg_n):
+        pl.semaphore_signal(barrier, inc=1, device_id=(seg_peer(d), q), device_id_type=MESH)
+    for d in range(1, seq_n):
+        pl.semaphore_signal(barrier, inc=1, device_id=(seg, seq_peer(d)), device_id_type=MESH)
+
+    order = [("peer", k) for k in range(chips)] + [("own", k) for k in range(chips)]
 
     def load(i):
         kind, k = order[i]
@@ -66,14 +76,18 @@
         pltpu.make_async_copy(w_value, wqkv.at[2], load_sem.at[n + 3]),
         pltpu.make_async_copy(w_out, wout, load_sem.at[n + 4]),
     ]
-    for i in range(min(AHEAD, n)):
+    small_loads = [
+        pltpu.make_async_copy(source, target, load_sem.at[n + 5 + i])
+        for i, (source, target) in enumerate((
+            (lengths_in, lengths_ref), (sections_in, sections_ref),
+            (live_in, live_ref), (gain_in, gain_ref)))
+    ]
+    for c in small_loads:
+        c.start()
+    for i in range(chips):
         load(i).start()
-
-    barrier = pltpu.get_barrier_semaphore()
-    for d in range(1, seg_n):
-        pl.semaphore_signal(barrier, inc=1, device_id=(seg_peer(d), q), device_id_type=MESH)
-    for d in range(1, seq_n):
-        pl.semaphore_signal(barrier, inc=1, device_id=(seg, seq_peer(d)), device_id_type=MESH)
+    for c in small_loads:
+        c.wait()
 
     len_row = lengths_ref[pl.ds(seg, 1), :].astype(f32)
     sec_row = sections_ref[pl.ds(seg, 1), :]
@@ -123,19 +137,22 @@
         return total
 
     for i, (kind, k) in enumerate(order):
-        if i + AHEAD < n:
-            load(i + AHEAD).start()
-        elif i + AHEAD == n:
+        if i < chips:
+            load(i + chips).start()
+        elif i == n - 2:
             for w in weight_loads:
                 w.start()
         load(i).wait()
         both = jnp.dot(weights[...], hid[i], preferred_element_type=f32)
         part = both[:sections] + both[sections:]
-        if i == 0:
-            pl.semaphore_wait(barrier, seg_n + seq_n - 2)
         if kind == "peer":
             pair_send[k] = part
-            pair_copy(k).start()
+            if k == chips // 2:
+                pl.semaphore_wait(barrier, seg_n + seq_n - 2)
+                for j in range(k):
+                    pair_copy(j).start()
+            if k >= chips // 2:
+                pair_copy(k).start()
             continue
         pair_copy(k).wait_recv()
         part = part + pair_recv[k]
@@ -163,12 +180,16 @@
     for d in range(1, seg_n):
         pool_copy(d).start()
     weight_loads[0].wait()
-    for d in range(1, seg_n):
-        pool_copy(d).wait_recv()
-    projected = jnp.dot(pooled[0], win[0:sub, :], preferred_element_type=f32)
+    for d in range(seg_n):
+        if d:
+            pool_copy(d).wait_recv()
+        slot = lax.rem(seg + seg_n - d, seg_n)
+        product[slot] = jnp.dot(
+            pooled[slot], win[pl.ds(pl.multiple_of(slot * sub, sub), sub), :],
+            preferred_element_type=f32)
+    projected = product[0]
     for s in range(1, seg_n):
-        projected += jnp.dot(
-            pooled[s], win[s * sub : (s + 1) * sub, :], preferred_element_type=f32)
+        projected += product[s]
     for s in range(seq_n):
         proj_send[s] = projected[s * here : (s + 1) * here, :].astype(bf16)
 
@@ -177,7 +198,7 @@
             proj_send.at[seq_peer(d)], proj_recv.at[q], proj_ss.at[d - 1], proj_rs.at[d - 1],
             device_id=(seg, seq_peer(d)), device_id_type=MESH)
 
-    for d in range(1, seq_n):
+    for d in far_first:
         proj_copy(d).start()
     proj_recv[q] = proj_send[q]
     for w in weight_loads[1:]:
@@ -204,7 +225,7 @@
             kv_send, kv_recv.at[q], kv_ss.at[d - 1], kv_rs.at[d - 1],
             device_id=(seg, seq_peer(d)), device_id_type=MESH)
 
-    for d in range(1, seq_n):
+    for d in far_first:
         kv_copy(d).start()
     kv_recv[q] = kv_send[...]
     queries = jnp.dot(normed, wqkv[0], preferred_element_type=f32).astype(bf16)
@@ -232,7 +253,7 @@
         attended.append(jnp.dot(probs, values, preferred_element_type=f32).astype(bf16))
     terms = jnp.dot(
         jnp.concatenate(attended, axis=1), wout[...], preferred_element_type=f32)
-    term_recv[seg] = terms
+    term_recv[seg] = terms.astype(bf16)
 
     def term_copy(d):
         return pltpu.make_async_remote_copy(
@@ -243,9 +264,9 @@
         term_copy(d).start()
     for d in range(1, seg_n):
         term_copy(d).wait_recv()
-    combined = term_recv[0]
+    combined = term_recv[0].astype(f32)
     for s in range(1, seg_n):
-        combined += term_recv[s]
+        combined += term_recv[s].astype(f32)
     out_ref[...] = (section_in + combined).astype(out_ref.dtype)
 
     for k in range(chips):
@@ -275,20 +296,24 @@
     width, columns = w_query.shape
     bf16, f32 = jnp.bfloat16, jnp.float32
     vmem = pl.BlockSpec(memory_space=pltpu.VMEM)
-    smem = pl.BlockSpec(memory_space=pltpu.SMEM)
     hbm = pl.BlockSpec(memory_space=pl.ANY)
     dma = pltpu.SemaphoreType.DMA
     kv = 2 * columns + HEAD_DIM
     return pl.pallas_call(
         functools.partial(kernel, seg_n, seq_n),
         out_shape=jax.ShapeDtypeStruct((here, width), bf16),
-        in_specs=[hbm, vmem, vmem, smem, vmem, hbm, hbm, hbm, hbm, hbm],
+        in_specs=[hbm] * 10,
         out_specs=vmem,
         scratch_shapes=[
+            pltpu.VMEM(span_lengths.shape, jnp.int32),
+            pltpu.VMEM(section_of.shape, jnp.int32),
+            pltpu.SMEM((here,), jnp.int32),
+            pltpu.VMEM((1, width), f32),
             pltpu.VMEM((seq_n, tokens, features), bf16),
             pltpu.VMEM(w_in.shape, bf16),
             pltpu.VMEM((3, width, columns), bf16),
             pltpu.VMEM(w_out.shape, bf16),
+            pltpu.VMEM((seg_n, sections, width), f32),
             pltpu.VMEM((2 * sections, tokens), bf16),
             pltpu.VMEM((chips, sections, features), f32),
             pltpu.VMEM((chips, sections, features), f32),
@@ -303,8 +328,8 @@
             pltpu.VMEM((here, kv), bf16),
             pltpu.VMEM((seq_n, here, kv), bf16),
             pltpu.VMEM((sections, kv), f32),
-            pltpu.VMEM((seg_n, here, width), f32),
-            dma((seq_n + 5,)),
+            pltpu.VMEM((seg_n, here, width), bf16),
+            dma((seq_n + 9,)),
             dma((chips,)), dma((chips,)),
             dma((chips, seg_n - 1)), dma((chips, seg_n - 1)),
             dma((chips - 1,)), dma((chips - 1,)),

time: 38.7 us -> 37.4 us (0.966)
  Pallas kernels: 37.1 us -> 35.8 us
    pallas_call x1, Pallas kernels: 37.1 us -> 35.8 us  [shards(): pl.pallas_call(functools.partial(kernel, seg_n, seq_n), out_shape=jax.Sha...]
where the time goes in v2:
time: 37.4 us; the launch traced here: 37.2 us
  Pallas kernels  35.8 us (96%)
  local copies, waits for them, and re-layouts  1.33 us (4%)
    pallas_call x1, Pallas kernels, shards(): pl.pallas_call(functools.partial(kernel, seg_n, seq_n), out_shape=jax.Sha...  35.8 us
    unnamed x1, local copies, waits for them, and re-layouts  1.33 us

profile of v2, /device:TPU:0, one launch (start us, length us, event | category | flops | bytes accessed | tf_op | source)
XLA Modules:
  0.0 37.2 jit_solution(15902686941429892302)
XLA Ops:
  0.0 35.8 %shard_map.100 = bf16[4,2048]{1,0:T(4,128)(2,1)} custom-call(bf16[1,1024,8192]{2,1,0:T(8,128)(2,1)} %hidden.1, s32[4,64]{1,0:T(4,128)} %lengths_in.1, s32[4,64]{1,0:T(4,128)} %sections_in.1, s32[4]{0:T(128)} %live_in.1, f32[1,2048]{1,0:T(1,128)} %bitcast.1, bf16[1024,2048]{1,0:T(8,128)(2,1)} %w_in.1, bf16[2048,512]{1,0:T(8,128)(2,1)} %w_query.1, ...), custom_call_target="tpu_custom_call" | custom-call | tf_op jit(solution)/shard_map/pallas_call | solution.py:302
  35.8 1.3 %copy.12 = bf16[4,2048]{1,0:T(4,128)(2,1)} copy(bf16[4,2048]{1,0:T(4,128)(2,1)} %shard_map.100) | data formatting | bytes 32768
